TPU v7x, 32 devices: a whole 2x2x4 slice. The times are simulated.
32 devices in a mesh: dp: 8 (over z, x), tensor: 4 (over y, core).
Axes of the slice: x: 2, y: 2, z: 4, core: 2. Of those that a mesh axis runs over, the one named last changes fastest.
Arguments:
- tokens: bfloat16 [32768, 768], P(('dp', 'tensor')), may hold values from -6 to 6
- cotangent: bfloat16 [32768, 768], P(('dp', 'tensor')), may hold values from -26 to 26
- seq_group: int32 [16], P('dp'), may hold values from 0 to 1
- block_slot: int32 [13830], replicated, may hold values from 0 to 20751, as said below
- master: float32 [4, 20752, 128], P('tensor', 'dp'), may hold values from -3 to 3
- first_moment: float32 [4, 20752, 128], P('tensor', 'dp'), may hold values from -1 to 1
- second_moment: float32 [4, 20752, 128], P('tensor', 'dp'), may hold values from 0 to 1, as said below
Outputs:
- output: bfloat16 [32768, 768], P(('dp', 'tensor'))
- input_grad: float32 [32768, 768], P(('dp', 'tensor'))
- group_norms: float32 [16], P('dp')
- new_master: float32 [4, 20752, 128], P('tensor', 'dp')
- new_first: float32 [4, 20752, 128], P('tensor', 'dp')
- new_second: float32 [4, 20752, 128], P('tensor', 'dp')
Inputs may be any that keep to these rules, and one draw needn't show every extreme that they name: `block_slot`: all entries differ; slot s belongs to the owner with dp index s // 2594; one owner holds 2594 blocks. `seq_group`: group ids count within one dp index: sequences of different dp indices never share a group. `second_moment`: Positive.
All inputs are finite; a program needn't handle non-finite values.
Results may differ from a plain program's by a relative error of at most 0.012.
Values may be sent and summed in bfloat16 or wider, within the bound.
No kernel may reach another device: no remote copies, remote signals or barrier semaphores. Data moves between devices by JAX's collectives and lax.ppermute only.
A program may use at most 256 MiB of HBM per device.

v0:
```python
import jax
import jax.numpy as jnp
from jax import lax
from jax.sharding import PartitionSpec as P

HEADS = 12
HD = 64
ROT = 16
FF = 3072
eps_norm = 1e-05
eps_adam = 1e-08
beta_one = 0.5
beta_two = 0.6
root_half = 0.7071067811865476
inv_root_tau = 0.3989422804014327


def rotary_tables(length, rot_dims):
    half_rot = rot_dims // 2
    frequency = 10000.0 ** (-2.0 * jnp.arange(half_rot, dtype=jnp.float32) / rot_dims)
    angles = jnp.arange(length, dtype=jnp.float32)[:, None] * frequency[None, :]
    return (jnp.cos(angles), jnp.sin(angles))


def rotate(features, cosine, sine_table, rot_dims):
    half_rot = rot_dims // 2
    first_half = features[..., :half_rot]
    second_half = features[..., half_rot:rot_dims]
    cos_cols = cosine[:, None, :]
    sin_cols = sine_table[:, None, :]
    return jnp.concatenate(
        [
            first_half * cos_cols - second_half * sin_cols,
            second_half * cos_cols + first_half * sin_cols,
            features[..., rot_dims:],
        ],
        axis=-1,
    )


def unrotate(grad_in, cosine, sine_table, rot_dims):
    half_rot = rot_dims // 2
    first_half = grad_in[..., :half_rot]
    second_half = grad_in[..., half_rot:rot_dims]
    cos_cols = cosine[:, None, :]
    sin_cols = sine_table[:, None, :]
    return jnp.concatenate(
        [
            first_half * cos_cols + second_half * sin_cols,
            second_half * cos_cols - first_half * sin_cols,
            grad_in[..., rot_dims:],
        ],
        axis=-1,
    )


def layer_norm(rows_in):
    row_mean = jnp.mean(rows_in, axis=-1, keepdims=True)
    centred = rows_in - row_mean
    inverse = lax.rsqrt(jnp.mean(centred * centred, axis=-1, keepdims=True) + eps_norm)
    return (centred * inverse, inverse)


def unpack(flat_params, d_model, heads_local, ff_local, width_local):
    inner_width = heads_local * HD
    end_qkv = d_model * 3 * inner_width
    end_out = end_qkv + inner_width * d_model
    end_up = end_out + d_model * ff_local
    end_down = end_up + ff_local * d_model
    return (
        flat_params[:end_qkv].reshape(d_model, 3 * inner_width),
        flat_params[end_qkv:end_out].reshape(inner_width, d_model),
        flat_params[end_out:end_up].reshape(d_model, ff_local),
        flat_params[end_up:end_down].reshape(ff_local, d_model),
        flat_params[end_down:].reshape(4, width_local),
    )


def step_rates(position, d_model, heads_local, head_dim, ff_local, seq_len, ff_all):
    end_qkv = d_model * 3 * heads_local * head_dim
    end_out = end_qkv + heads_local * head_dim * d_model
    end_up = end_out + d_model * ff_local
    end_down = end_up + ff_local * d_model
    matrix_rate = d_model ** (-0.5)
    learn_rate = jnp.where(
        position < end_qkv,
        matrix_rate,
        jnp.where(
            position < end_out,
            (seq_len / (5.0 * d_model)) ** 0.5,
            jnp.where(
                position < end_up,
                matrix_rate,
                jnp.where(position < end_down, ff_all ** (-0.5), 0.1),
            ),
        ),
    )
    weight_decay = jnp.where(position < end_down, 0.1, 0.0)
    return (learn_rate.astype(jnp.float32), weight_decay.astype(jnp.float32))


def adam_update(weight, moment_one, moment_two, gradient, learn_rate, weight_decay):
    new_one = beta_one * moment_one + (1.0 - beta_one) * gradient
    new_two = beta_two * moment_two + (1.0 - beta_two) * gradient * gradient
    new_weight = weight - learn_rate * (
        new_one / (jnp.sqrt(new_two) + eps_adam) + weight_decay * weight
    )
    return (new_weight, new_one, new_two)


def by_sequence(tensor_in, seq_count):
    return tensor_in.reshape(seq_count, -1, tensor_in.shape[-1])


def seq_product(left, right, seq_count):
    return jnp.einsum(
        "sli,slj->sij",
        by_sequence(left, seq_count),
        by_sequence(right, seq_count),
        preferred_element_type=jnp.float32,
    )


def on_device(tokens, cotangent, seq_group, block_slot, master, first_moment, second_moment):
    tensor_count = lax.axis_size("tensor")
    tensor_rank = lax.axis_index("tensor")
    owner_index = lax.axis_index("dp")
    owner_count = lax.axis_size("dp")
    d_model = tokens.shape[1]
    local_rows = tokens.shape[0]
    width_local = d_model // tensor_count
    heads_local = HEADS // tensor_count
    inner_width = heads_local * HD
    ff_local = FF // tensor_count
    seq_count = seq_group.shape[0]
    tok_count = local_rows * tensor_count
    seq_len = tok_count // seq_count
    capacity = master.shape[1]
    block_width = master.shape[2]
    block_count = block_slot.shape[0]
    copies = lax.all_gather(master[0].astype(jnp.bfloat16), "dp", axis=0, tiled=True)
    flat_params = copies[block_slot].reshape(-1)
    w_qkv, w_out, w_up, w_down, norm_local = unpack(
        flat_params, d_model, heads_local, ff_local, width_local
    )
    x_full, norm_rows = (
        lax.all_gather(tokens, "tensor", axis=0, tiled=True),
        lax.all_gather(norm_local.reshape(1, 4 * width_local), "tensor", axis=0, tiled=True),
    )
    norm_full = jnp.transpose(norm_rows.reshape(tensor_count, 4, width_local), (1, 0, 2)).reshape(
        4, d_model
    )
    rows_full = x_full.astype(jnp.float32)
    normed, inverse = layer_norm(rows_full)
    norm_gains = norm_full.astype(jnp.float32)
    first_in = (normed * norm_gains[0] + norm_gains[1]).astype(jnp.bfloat16)
    second_in = (normed * norm_gains[2] + norm_gains[3]).astype(jnp.bfloat16)
    projected = jnp.dot(first_in, w_qkv, preferred_element_type=jnp.float32).reshape(
        seq_count, seq_len, 3, heads_local, HD
    )
    cosine, sine_table = rotary_tables(seq_len, ROT)
    queries = rotate(projected[:, :, 0], cosine, sine_table, ROT).astype(jnp.bfloat16)
    key_rows = rotate(projected[:, :, 1], cosine, sine_table, ROT).astype(jnp.bfloat16)
    values = projected[:, :, 2].astype(jnp.bfloat16)
    block_rows = min(512, seq_len)
    block_total = seq_len // block_rows
    scale_factor = HD ** (-0.5)
    starts = jnp.arange(block_total, dtype=jnp.int32) * block_rows
    key_index = jnp.arange(seq_len, dtype=jnp.int32)

    def scores_of(row_start):
        query_block = lax.dynamic_slice_in_dim(queries, row_start, block_rows, 1)
        scores = (
            jnp.einsum("sqhd,skhd->shqk", query_block, key_rows, preferred_element_type=jnp.float32)
            * scale_factor
        )
        allowed = (row_start + jnp.arange(block_rows, dtype=jnp.int32))[:, None] >= key_index[
            None, :
        ]
        return (jnp.where(allowed, scores, -1e30), query_block)

    def forward_block(row_start):
        scores = scores_of(row_start)[0]
        row_peak = jnp.max(scores, axis=-1, keepdims=True)
        exp_scores = jnp.exp(scores - row_peak)
        row_total = jnp.sum(exp_scores, axis=-1, keepdims=True)
        weights_low = (exp_scores / row_total).astype(jnp.bfloat16)
        mixed_heads = jnp.einsum(
            "shqk,skhd->sqhd", weights_low, values, preferred_element_type=jnp.float32
        )
        return (mixed_heads, row_peak + jnp.log(row_total))

    mixed_heads, log_sums = lax.map(forward_block, starts)
    attended = jnp.moveaxis(mixed_heads, 0, 1).reshape(tok_count, inner_width).astype(jnp.bfloat16)
    hidden_pre = jnp.dot(second_in, w_up, preferred_element_type=jnp.float32)
    hidden_low = jax.nn.gelu(hidden_pre, approximate=False).astype(jnp.bfloat16)
    branch = jnp.dot(attended, w_out, preferred_element_type=jnp.float32) + jnp.dot(
        hidden_low, w_down, preferred_element_type=jnp.float32
    )
    branch_sum = lax.psum_scatter(
        branch.astype(jnp.bfloat16), "tensor", scatter_dimension=0, tiled=True
    ).astype(jnp.float32)
    output = (tokens.astype(jnp.float32) + branch_sum).astype(jnp.bfloat16)
    back_full = lax.all_gather(cotangent, "tensor", axis=0, tiled=True)
    grad_down = seq_product(hidden_low, back_full, seq_count)
    grad_hidden = jnp.dot(back_full, w_down.T, preferred_element_type=jnp.float32)
    cumulative = 0.5 * (1.0 + lax.erf(hidden_pre * root_half))
    density = jnp.exp(-0.5 * hidden_pre * hidden_pre) * inv_root_tau
    grad_pre = (grad_hidden * (cumulative + hidden_pre * density)).astype(jnp.bfloat16)
    grad_up = seq_product(second_in, grad_pre, seq_count)
    second_back = jnp.dot(grad_pre, w_up.T, preferred_element_type=jnp.float32)
    grad_out = seq_product(attended, back_full, seq_count)
    grad_attended = jnp.dot(back_full, w_out.T, preferred_element_type=jnp.float32).astype(
        jnp.bfloat16
    )
    grad_blocks_in = jnp.moveaxis(
        grad_attended.reshape(seq_count, block_total, block_rows, heads_local, HD), 1, 0
    )

    def backward_block(carried, inputs):
        row_start, log_sum, grad_block = inputs
        scores, query_block = scores_of(row_start)
        probs = jnp.exp(scores - log_sum)
        grad_probs = jnp.einsum(
            "sqhd,skhd->shqk", grad_block, values, preferred_element_type=jnp.float32
        )
        row_dot = jnp.sum(probs * grad_probs, axis=-1, keepdims=True)
        grad_scores = (probs * (grad_probs - row_dot)).astype(jnp.bfloat16)
        grad_query = (
            jnp.einsum("shqk,skhd->sqhd", grad_scores, key_rows, preferred_element_type=jnp.float32)
            * scale_factor
        )
        grad_keys = (
            carried[0]
            + jnp.einsum(
                "shqk,sqhd->skhd", grad_scores, query_block, preferred_element_type=jnp.float32
            )
            * scale_factor
        )
        grad_values = carried[1] + jnp.einsum(
            "shqk,sqhd->skhd",
            probs.astype(jnp.bfloat16),
            grad_block,
            preferred_element_type=jnp.float32,
        )
        return ((grad_keys, grad_values), grad_query)

    zero_heads = jnp.zeros((seq_count, seq_len, heads_local, HD), jnp.float32)
    key_value_grads, grad_queries = lax.scan(
        backward_block, (zero_heads, zero_heads), (starts, log_sums, grad_blocks_in)
    )
    grad_queries = jnp.moveaxis(grad_queries, 0, 1).reshape(seq_count, seq_len, heads_local, HD)
    grad_qkv = (
        jnp.stack(
            [
                unrotate(grad_queries, cosine, sine_table, ROT),
                unrotate(key_value_grads[0], cosine, sine_table, ROT),
                key_value_grads[1],
            ],
            axis=2,
        )
        .reshape(tok_count, 3 * inner_width)
        .astype(jnp.bfloat16)
    )
    grad_qkv_w = seq_product(first_in, grad_qkv, seq_count)
    first_back = jnp.dot(grad_qkv, w_qkv.T, preferred_element_type=jnp.float32)
    row_start_local = tensor_rank * local_rows
    first_sum, second_sum = (
        lax.psum_scatter(
            first_back.astype(jnp.bfloat16), "tensor", scatter_dimension=0, tiled=True
        ).astype(jnp.float32),
        lax.psum_scatter(
            second_back.astype(jnp.bfloat16), "tensor", scatter_dimension=0, tiled=True
        ).astype(jnp.float32),
    )
    normed_rows = lax.dynamic_slice_in_dim(normed, row_start_local, local_rows, 0)
    inverse_rows = lax.dynamic_slice_in_dim(inverse, row_start_local, local_rows, 0)
    scaled_first = first_sum * norm_gains[0]
    scaled_second = second_sum * norm_gains[2]
    first_mean = jnp.mean(scaled_first, axis=1, keepdims=True)
    first_cross = jnp.mean(scaled_first * normed_rows, axis=1, keepdims=True)
    second_mean = jnp.mean(scaled_second, axis=1, keepdims=True)
    second_cross = jnp.mean(scaled_second * normed_rows, axis=1, keepdims=True)
    grad_input = (
        cotangent.astype(jnp.float32)
        + inverse_rows * (scaled_first - first_mean - normed_rows * first_cross)
        + inverse_rows * (scaled_second - second_mean - normed_rows * second_cross)
    )
    row_seq = (row_start_local + jnp.arange(local_rows, dtype=jnp.int32)) // seq_len
    row_member = (row_seq[None, :] == jnp.arange(seq_count, dtype=jnp.int32)[:, None]).astype(
        jnp.float32
    )
    partial_sums = jnp.stack(
        [
            jnp.dot(row_member, first_sum * normed_rows, precision=lax.Precision.HIGHEST),
            jnp.dot(row_member, first_sum, precision=lax.Precision.HIGHEST),
            jnp.dot(row_member, second_sum * normed_rows, precision=lax.Precision.HIGHEST),
            jnp.dot(row_member, second_sum, precision=lax.Precision.HIGHEST),
        ],
        axis=1,
    )
    norm_grads = lax.psum_scatter(partial_sums, "tensor", scatter_dimension=2, tiled=True)
    per_seq = jnp.concatenate(
        [
            grad_qkv_w.reshape(seq_count, -1),
            grad_out.reshape(seq_count, -1),
            grad_up.reshape(seq_count, -1),
            grad_down.reshape(seq_count, -1),
            norm_grads.reshape(seq_count, -1),
        ],
        axis=1,
    )
    member = (seq_group[None, :] == jnp.arange(seq_count, dtype=jnp.int32)[:, None]).astype(
        jnp.float32
    )
    group_grads = jnp.dot(member, per_seq, precision=lax.Precision.HIGHEST)
    squares = lax.psum(jnp.sum(group_grads * group_grads, axis=1), "tensor")
    group_norms = jnp.sqrt(squares)
    clip_scale = 1.0 / jnp.maximum(group_norms, 1.0)
    clipped = jnp.dot(clip_scale, group_grads, precision=lax.Precision.HIGHEST)
    grad_rows = clipped.reshape(block_count, block_width)
    slot_total = owner_count * capacity
    slot_block = (
        jnp.full((slot_total,), -1, jnp.int32)
        .at[block_slot]
        .set(jnp.arange(block_count, dtype=jnp.int32))
    )
    my_blocks = lax.dynamic_slice_in_dim(slot_block, owner_index * capacity, capacity)
    summed = lax.psum(grad_rows, "dp")
    owned_grad = jnp.where(my_blocks[:, None] >= 0, summed[jnp.maximum(my_blocks, 0)], 0.0)
    position = (
        jnp.maximum(my_blocks, 0)[:, None] * block_width
        + jnp.arange(block_width, dtype=jnp.int32)[None, :]
    )
    learn_rate, weight_decay = step_rates(position, d_model, heads_local, HD, ff_local, seq_len, FF)
    new_weight, new_one, new_two = adam_update(
        master[0], first_moment[0], second_moment[0], owned_grad, learn_rate, weight_decay
    )
    return (output, grad_input, group_norms, new_weight[None], new_one[None], new_two[None])


def solution(mesh):
    placed = (
        P(("dp", "tensor"), None),
        P(("dp", "tensor"), None),
        P("dp"),
        P(),
        P("tensor", "dp", None),
        P("tensor", "dp", None),
        P("tensor", "dp", None),
    )
    return jax.shard_map(
        on_device,
        mesh=mesh,
        in_specs=placed,
        out_specs=(
            P(("dp", "tensor"), None),
            P(("dp", "tensor"), None),
            P("dp"),
            P("tensor", "dp", None),
            P("tensor", "dp", None),
            P("tensor", "dp", None),
        ),
        check_vma=False,
    )
```

profile of v0, /device:TPU:0, one launch (start us, length us, event | category | flops | bytes accessed | tf_op | source)
XLA Modules:
  0.0 1451.3 jit_solution(10674566761597092681)
XLA Ops:
  17.1 148.8 %all-gather.10.cloned.1.call-done = bf16[1,20752,128]{2,0,1:T(2,128)(2,1)} async-done(((bf16[1,2594,128]{2,0,1:T(2,128)(2,1)}), bf16[1,20752,128]{2,0,1:T(2,128)(2,1)}) %all-gather.10.cloned.1.call-update) | async-done | bytes 5312528 | tf_op jit(solution)/shard_map/all_gather | solution.py:141
  165.9 8.5 copy.115
  174.4 30.7 %gather_fusion = bf16[13830,128]{1,0:T(8,128)(2,1)S(1)} fusion(bf16[20752,128]{1,0:T(8,128)(2,1)} %bitcast.203, s32[14336]{0:T(1024)} %pad_clamp_fusion), kind=kCustom, calls=%fused_computation | custom fusion | bytes 7136280 | tf_op jit(solution)/shard_map/gather | solution.py:142
  234.9 7.9 fusion.36
  250.1 10.0 all-gather.8.cloned.1.call-done
  260.0 6.1 fusion.55
  276.1 163.2 %while.30 = (s32[]{:T(128)}, bf16[4,2,512,3,64]{2,4,3,1,0:T(8,128)(2,1)}, f32[4,2,3,512,1]{3,2,1,4,0:T(4,128)S(1)}, s32[4]{0:T(128)S(1)}, bf16[2,2048,3,64]{1,3,...) while((s32[]{:T(128)}, ...), condition=%wide.region_5.6_spmd.clone.clone, body=%wide.region_2.5_spmd.clone.sunk.clone | while | flops 1687156224 | bytes 96723152 | solution.py:193
  280.0 12.1 fusion.178
  292.1 12.1 fusion.179
  304.2 11.6 fusion.180
  320.8 12.1 fusion.178
  332.9 12.1 fusion.179
  345.0 11.6 fusion.180
  361.6 12.1 fusion.178
  373.7 12.1 fusion.179
  385.8 11.6 fusion.180
  402.4 12.1 fusion.178
  414.5 12.1 fusion.179
  426.6 11.6 fusion.180
  439.3 336.2 %while.31 = (s32[]{:T(128)}, f32[2,2048,3,64]{1,3,2,0:T(8,128)}, f32[2,2048,3,64]{1,3,2,0:T(8,128)}, f32[4,2,512,3,64]{2,4,3,1,0:T(8,128)}, s32[4]{0:T(128)S(1)}...) while((s32[]{:T(128)}, f32[2,2048,3,64]{1,3,2,0:T(8,128)}, ...), condition=%wide.region_9.10_spmd.clone.clone, body=%wide.region_7.9_spmd.clone.sunk.clone | while | flops 4126078464 | bytes 275603712 | solution.py:249
  443.5 11.3 fusion.190
  454.8 12.9 bitcast_add_fusion.7
  467.7 18.1 %multiply_reduce_fusion.4 = (f32[2,3,512]{2,1,0:T(4,128)S(1)}, f32[2,3,512,2048]{3,2,1,0:T(8,128)}) fusion(f32[2,3,512,2048]{3,2,1,0:T(8,128)} %fusion.190, f32[2,3,512]{2,1,0:T(4,128)S(1)} %dynamic-slice_bitcast_fusion.3, pred[512,2048]{1,0:T(8,128)(4,1)S(1)} %iota_compare_fusion.12, bf16[2,2048,3,64]{1,3,2,0:T(8,128)(2,1)} %copy-done.1, ...), kind=kOutput, calls=%fused_computation.22.clone.1.clone | convolution fusion | flops 836760576 | bytes 53370884 | tf_op jit(solution)/shard_map/while/body/eval_jaxpr/sqhd,skhd->shqk/dot_general | solution.py:224
  485.8 17.0 %multiply_convert_fusion.3 = bf16[2,3,512,2048]{3,2,1,0:T(8,128)(2,1)S(1)} fusion(f32[2,3,512,2048]{3,2,1,0:T(8,128)} %get-tuple-element.409, f32[2,3,512,2048]{3,2,1,0:T(8,128)} %fusion.190, f32[2,3,512]{2,1,0:T(4,128)S(1)} %get-tuple-element.410, f32[2,3,512]{2,1,0:T(4,128)S(1)} %dynamic-slice_bitcast_fusion.3, ...), kind=kLoop, calls=%fused_computation.21.clone.1.clone | loop fusion | flops 37748736 | bytes 63987712 | tf_op jit(solution)/shard_map/while/body/eval_jaxpr/convert_element_type | solution.py:228
  512.5 9.5 fusion.191
  526.0 11.3 fusion.190
  537.3 13.8 bitcast_add_fusion.7
  551.1 18.1 %multiply_reduce_fusion.4 = (f32[2,3,512]{2,1,0:T(4,128)S(1)}, f32[2,3,512,2048]{3,2,1,0:T(8,128)}) fusion(f32[2,3,512,2048]{3,2,1,0:T(8,128)} %fusion.190, f32[2,3,512]{2,1,0:T(4,128)S(1)} %dynamic-slice_bitcast_fusion.3, pred[512,2048]{1,0:T(8,128)(4,1)S(1)} %iota_compare_fusion.12, bf16[2,2048,3,64]{1,3,2,0:T(8,128)(2,1)} %copy-done.1, ...), kind=kOutput, calls=%fused_computation.22.clone.1.clone | convolution fusion | flops 836760576 | bytes 53370884 | tf_op jit(solution)/shard_map/while/body/eval_jaxpr/sqhd,skhd->shqk/dot_general | solution.py:224
  569.2 17.0 %multiply_convert_fusion.3 = bf16[2,3,512,2048]{3,2,1,0:T(8,128)(2,1)S(1)} fusion(f32[2,3,512,2048]{3,2,1,0:T(8,128)} %get-tuple-element.409, f32[2,3,512,2048]{3,2,1,0:T(8,128)} %fusion.190, f32[2,3,512]{2,1,0:T(4,128)S(1)} %get-tuple-element.410, f32[2,3,512]{2,1,0:T(4,128)S(1)} %dynamic-slice_bitcast_fusion.3, ...), kind=kLoop, calls=%fused_computation.21.clone.1.clone | loop fusion | flops 37748736 | bytes 63987712 | tf_op jit(solution)/shard_map/while/body/eval_jaxpr/convert_element_type | solution.py:228
  590.8 6.1 bitcast_add_fusion.6
  596.9 9.5 fusion.191
  610.4 11.3 fusion.190
  621.7 13.8 bitcast_add_fusion.7
  635.5 18.1 %multiply_reduce_fusion.4 = (f32[2,3,512]{2,1,0:T(4,128)S(1)}, f32[2,3,512,2048]{3,2,1,0:T(8,128)}) fusion(f32[2,3,512,2048]{3,2,1,0:T(8,128)} %fusion.190, f32[2,3,512]{2,1,0:T(4,128)S(1)} %dynamic-slice_bitcast_fusion.3, pred[512,2048]{1,0:T(8,128)(4,1)S(1)} %iota_compare_fusion.12, bf16[2,2048,3,64]{1,3,2,0:T(8,128)(2,1)} %copy-done.1, ...), kind=kOutput, calls=%fused_computation.22.clone.1.clone | convolution fusion | flops 836760576 | bytes 53370884 | tf_op jit(solution)/shard_map/while/body/eval_jaxpr/sqhd,skhd->shqk/dot_general | solution.py:224
  653.6 17.0 %multiply_convert_fusion.3 = bf16[2,3,512,2048]{3,2,1,0:T(8,128)(2,1)S(1)} fusion(f32[2,3,512,2048]{3,2,1,0:T(8,128)} %get-tuple-element.409, f32[2,3,512,2048]{3,2,1,0:T(8,128)} %fusion.190, f32[2,3,512]{2,1,0:T(4,128)S(1)} %get-tuple-element.410, f32[2,3,512]{2,1,0:T(4,128)S(1)} %dynamic-slice_bitcast_fusion.3, ...), kind=kLoop, calls=%fused_computation.21.clone.1.clone | loop fusion | flops 37748736 | bytes 63987712 | tf_op jit(solution)/shard_map/while/body/eval_jaxpr/convert_element_type | solution.py:228
  675.2 6.1 bitcast_add_fusion.6
  681.3 9.5 fusion.191
  694.8 11.3 fusion.190
  706.1 13.8 bitcast_add_fusion.7
  719.9 18.1 %multiply_reduce_fusion.4 = (f32[2,3,512]{2,1,0:T(4,128)S(1)}, f32[2,3,512,2048]{3,2,1,0:T(8,128)}) fusion(f32[2,3,512,2048]{3,2,1,0:T(8,128)} %fusion.190, f32[2,3,512]{2,1,0:T(4,128)S(1)} %dynamic-slice_bitcast_fusion.3, pred[512,2048]{1,0:T(8,128)(4,1)S(1)} %iota_compare_fusion.12, bf16[2,2048,3,64]{1,3,2,0:T(8,128)(2,1)} %copy-done.1, ...), kind=kOutput, calls=%fused_computation.22.clone.1.clone | convolution fusion | flops 836760576 | bytes 53370884 | tf_op jit(solution)/shard_map/while/body/eval_jaxpr/sqhd,skhd->shqk/dot_general | solution.py:224
  738.0 17.0 %multiply_convert_fusion.3 = bf16[2,3,512,2048]{3,2,1,0:T(8,128)(2,1)S(1)} fusion(f32[2,3,512,2048]{3,2,1,0:T(8,128)} %get-tuple-element.409, f32[2,3,512,2048]{3,2,1,0:T(8,128)} %fusion.190, f32[2,3,512]{2,1,0:T(4,128)S(1)} %get-tuple-element.410, f32[2,3,512]{2,1,0:T(4,128)S(1)} %dynamic-slice_bitcast_fusion.3, ...), kind=kLoop, calls=%fused_computation.21.clone.1.clone | loop fusion | flops 37748736 | bytes 63987712 | tf_op jit(solution)/shard_map/while/body/eval_jaxpr/convert_element_type | solution.py:228
  765.7 9.5 fusion.191
  788.4 9.5 copy.74
  813.7 9.7 fusion.108
  828.9 9.4 convolution_convert_fusion
  840.7 33.3 %fusion.41 = (bf16[4096,768]{1,0:T(8,128)(2,1)}, f32[4096,768]{1,0:T(8,128)S(1)}) fusion(bf16[4096,768]{1,0:T(8,128)(2,1)} %get-tuple-element.243, bf16[768,768]{1,0:T(8,128)(2,1)S(1)} %copy-done.22), kind=kOutput, calls=%fused_computation.59 | convolution fusion | flops 5036310528 | bytes 26345472 | tf_op jit(solution)/shard_map/dot_general | solution.py:195
  874.0 9.2 fusion.47
  885.8 7.0 convolution_convert_fusion.1
  892.8 9.4 convolution_bitcast_fusion.1
  909.1 6.2 constant_dynamic-update-slice_fusion.2
  917.7 12.2 convolution_bitcast_fusion
  929.9 11.5 fusion.107
  946.8 21.3 %reduce-scatter.11.cloned.1.call-done = bf16[1024,768]{1,0:T(8,128)(2,1)} async-done(((bf16[4096,768]{1,0:T(8,128)(2,1)}), bf16[1024,768]{1,0:T(8,128)(2,1)}) %reduce-scatter.11.cloned.1.call-update) | async-done | bytes 1572880 | tf_op jit(solution)/shard_map/reduce_scatter | solution.py:272
  977.0 9.1 add_convert_fusion
  986.1 8.1 copy.103
  1002.3 41.5 %multiply_reduce_fusion.1 = (f32[2]{0:T(128)S(1)}, f32[2,1770240]{1,0:T(2,128)}) fusion(f32[2,1770240]{1,0:T(2,128)} %constant_dynamic-update-slice_fusion, s32[2]{0:T(128)S(1)} %copy-done.37), kind=kOutput, calls=%fused_computation.55 | convolution fusion | flops 92052480 | bytes 28323856 | tf_op jit(solution)/shard_map/dot_general | solution.py:316
  1043.8 6.4 psum.14
  1050.1 119.3 %convolution_reduce_fusion = f32[1770240]{0:T(1024)} fusion(f32[2,1770240]{1,0:T(2,128)} %get-tuple-element.263, f32[2]{0:T(128)S(1)} %sqrt.7), kind=kOutput, calls=%fused_computation.116 | convolution fusion | flops 42485764 | bytes 21242888 | tf_op jit(solution)/shard_map/dot_general | solution.py:320
  1169.4 65.6 %scatter_custom_fusion = s32[20752]{0:T(1024)S(1)} fusion(s32[13830]{0:T(1024)} %copy-done.27, s32[13830]{0:T(1024)S(1)} %iota.92, s32[]{:T(128)} %constant.72.clone.1), kind=kCustom, calls=%fused_computation.158 | custom fusion | bytes 83520 | tf_op jit(solution)/shard_map/scatter | solution.py:326
  1246.7 157.5 %all-reduce.2.cloned.1.call-done = f32[13830,128]{1,0:T(8,128)} async-done(((f32[13830,128]{1,0:T(8,128)}), f32[13830,128]{1,0:T(8,128)}) %all-reduce.2.cloned.1.call-update) | async-done | bytes 7080976 | tf_op jit(solution)/shard_map/psum | solution.py:329
  1404.2 7.7 gather_fusion.1
  1417.1 9.0 copy.86
  1426.1 9.0 copy.88
  1435.1 9.0 copy.87
  (270 shorter events, 193.2 us)
Async XLA Ops:
  7.2 7.7 copy-start.35
  7.2 158.7 %all-gather.10.cloned.1.call-start = ((), (), s32[]{:S(2)}) async-start(), calls=%async_computation.10 | async-start | bytes 11953152 | tf_op jit(solution)/shard_map/all_gather | solution.py:141
  10.8 217.5 %all-gather.6.cloned.1.call-start = ((), (), s32[]{:S(2)}) async-start(), calls=%async_computation.4 | async-start | bytes 7864320 | tf_op jit(solution)/shard_map/all_gather | solution.py:147
  11.6 248.4 %all-gather.8.cloned.1.call-start = ((), (), s32[]{:S(2)}) async-start(), calls=%async_computation.6 | async-start | bytes 7864320 | tf_op jit(solution)/shard_map/all_gather | solution.py:204
  12.3 929.1 %reduce-scatter.9.cloned.1.call-start = ((), (), s32[]{:S(2)}) async-start(), calls=%async_computation.7 | async-start | bytes 7864320 | tf_op jit(solution)/shard_map/reduce_scatter | solution.py:269
  214.3 20.6 %copy-start.31 = (f32[768]{0:T(1024)}, f32[768]{0:T(1024)S(1)}, u32[]{:S(2)}) copy-start(f32[768]{0:T(1024)S(1)} %mul.459) | copy-start | bytes 9220
  214.4 20.5 %copy-start.33 = (f32[768]{0:T(1024)}, f32[768]{0:T(1024)S(1)}, u32[]{:S(2)}) copy-start(f32[768]{0:T(1024)S(1)} %mul.475) | copy-start | bytes 9220
  220.0 6.4 copy-start.16
  225.8 6.4 copy-start.17
  228.3 4.7 copy-start.3
  232.2 2.7 copy-start.36
  234.9 7.9 copy-start.30
  242.8 3.9 copy-start.12
  246.9 13.1 copy-start.18
  269.5 3.6 copy-start.11
  269.5 3.8 copy-start.23
  269.5 3.8 copy-start.25
  273.3 2.8 copy-start.29
  273.3 2.8 copy-start.39
  292.1 12.1 copy-start.7
  332.9 12.1 copy-start.7
  373.7 12.1 copy-start.7
  414.5 12.1 copy-start.7
  439.5 3.3 copy-start.1
  502.9 4.5 copy-start
  512.5 9.5 copy-start.2
  522.0 3.3 copy-start.1
  586.3 4.5 copy-start
  596.9 9.5 copy-start.2
  606.4 3.3 copy-start.1
  670.7 4.5 copy-start
  681.3 9.5 copy-start.2
  690.9 3.3 copy-start.1
  755.1 4.5 copy-start
  765.7 9.5 copy-start.2
  775.6 4.1 copy-start.24
  775.6 4.1 copy-start.26
  788.4 9.5 copy-start.9
  799.1 9.3 slice-start
  801.7 6.7 slice-start.1
  806.5 7.2 slice-start.4
  808.4 5.2 slice-start.5
  838.3 129.8 %reduce-scatter.11.cloned.1.call-start = ((), (), s32[]{:S(2)}) async-start(), calls=%async_computation.8 | async-start | bytes 7864320 | tf_op jit(solution)/shard_map/reduce_scatter | solution.py:272
  838.3 35.7 %slice-start.2 = ((s8[6291456]{0:T(1024)(128)(4,1)}), s8[4194304]{0:T(1024)(128)(4,1)S(1)}, s32[]{:S(2)}) async-start(s8[6291456]{0:T(1024)(128)(4,1)} %bitcast.218), calls=%async_computation.14 | async-start | bytes 8388608
  840.6 33.3 %slice-start.3 = ((s8[6291456]{0:T(1024)(128)(4,1)}), s8[2097152]{0:T(1024)(128)(4,1)S(1)}, s32[]{:S(2)}) async-start(s8[6291456]{0:T(1024)(128)(4,1)} %bitcast.218), calls=%async_computation.15 | async-start | bytes 4194304
  840.7 33.3 %copy-start.20 = (bf16[768,768]{1,0:T(8,128)(2,1)S(1)}, bf16[768,768]{1,0:T(8,128)(2,1)}, u32[]{:S(2)}) copy-start(bf16[768,768]{1,0:T(8,128)(2,1)} %reshape.377) | copy-start | bytes 3538948
  883.2 2.6 copy-start.38
  902.2 5.8 copy-start.15
  909.1 91.2 %reduce-scatter.13.cloned.1.call-start = ((), (), s32[]{:S(2)}) async-start(), calls=%async_computation.11 | async-start | bytes 491520
  909.1 6.2 copy-start.10
  917.7 12.2 copy-start.21
  929.9 11.5 copy-start.28
  946.8 30.2 %copy-start.19 = (bf16[192,768]{1,0:T(8,128)(2,1)S(1)}, bf16[192,768]{1,0:T(8,128)(2,1)}, u32[]{:S(2)}) copy-start(bf16[192,768]{1,0:T(8,128)(2,1)} %reshape.375) | copy-start | bytes 884740
  968.1 3.8 copy-start.6
  976.5 262.1 %reduce-scatter.7.cloned.1.call-start = ((), (), s32[]{:S(2)}) async-start(), calls=%async_computation.5 | async-start | bytes 7864320 | tf_op jit(solution)/shard_map/reduce_scatter | solution.py:200
  994.2 410.0 %all-reduce.2.cloned.1.call-start = ((), (), s32[]{:S(2)}) async-start(), calls=%async_computation.9 | async-start | bytes 14163968 | tf_op jit(solution)/shard_map/psum | solution.py:329
  994.3 8.0 copy-start.37
  1050.1 119.3 %copy-start.40 = (f32[2]{0:T(128)}, f32[2]{0:T(128)S(1)}, u32[]{:S(2)}) copy-start(f32[2]{0:T(128)S(1)} %sqrt.7) | copy-start | bytes 28
  1169.4 65.9 %copy-start.5 = (bf16[1024,768]{1,0:T(8,128)(2,1)S(1)}, bf16[1024,768]{1,0:T(8,128)(2,1)}, u32[]{:S(2)}) copy-start(bf16[1024,768]{1,0:T(8,128)(2,1)} %reduce-scatter.9.cloned.1.call-done) | copy-start | bytes 4718596
  1169.4 65.9 %copy-start.32 = (f32[768]{0:T(1024)S(1)}, f32[768]{0:T(1024)}, u32[]{:S(2)}) copy-start(f32[768]{0:T(1024)} %copy-done.31) | copy-start | bytes 9220
  1169.4 65.9 %copy-start.34 = (f32[768]{0:T(1024)S(1)}, f32[768]{0:T(1024)}, u32[]{:S(2)}) copy-start(f32[768]{0:T(1024)} %copy-done.33) | copy-start | bytes 9220
  1235.3 7.0 dynamic-slice-start
  1238.6 3.6 copy-start.13
  1246.7 165.3 %copy-start.14 = (f32[1,2594,128]{2,0,1:T(1,128)S(1)}, f32[1,2594,128]{2,0,1:T(1,128)}, u32[]{:S(2)}) copy-start(f32[1,2594,128]{2,0,1:T(1,128)} %param.15) | copy-start | bytes 3984388
  (7 other events, 9.8 us)
Sparse Core Ops, SparseCore 0:
  10.9 154.8 all-gather.9
  167.4 44.5 all-gather.5
  213.6 46.4 all-gather.7
  838.4 58.8 reduce-scatter.8
  909.2 58.8 reduce-scatter.10
  976.7 20.7 reduce-scatter.12
  1000.0 58.9 reduce-scatter.6
  1169.5 234.6 all-reduce.1
where the time goes:
time: 1460 us; the launch traced here: 1450 us
  matrix products  624 us (43%)
  waiting for transfers between devices  339 us (23%)
  local copies, waits for them, and re-layouts  273 us (19%)
  other arithmetic  172 us (12%)
  loops' own time  16.5 us (1%)
  between operations  15.2 us (1%)
    psum x1, waiting for transfers between devices, on_device(): summed = lax.psum(grad_rows, 'dp')  158 us
    all_gather x1, waiting for transfers between devices, on_device(): lax.all_gather(master[0].astype(jnp.bfloat16), 'dp', axis=0, tiled=True)  149 us
    dot_general x1, matrix products, on_device(): clipped = jnp.dot(clip_scale, group_grads, precision=lax.Precision.HIGHEST)  119 us
    dot_general x8, matrix products, scores_of(): jnp.einsum('sqhd,skhd->shqk', query_block, key_rows, preferred_element_ty...  93.7 us
    unnamed x100, local copies, waits for them, and re-layouts  83.8 us
    dot_general x4, matrix products, backward_block(): jnp.einsum('sqhd,skhd->shqk', grad_block, values, preferred_element_type=...  72.5 us
    convert_element_type x4, other arithmetic, backward_block(): grad_scores = (probs * (grad_probs - row_dot)).astype(jnp.bfloat16)  68.2 us
    scatter x1, local copies, waits for them, and re-layouts, on_device(): slot_block = jnp.full((slot_total,), -1, jnp.int32).at[block_slot].set(jn...  65.6 us
  transfers between devices with their start and end apart: 8, of which 4 were waited for; matrix products, arithmetic and copies ran while one was open for 31% of the time, Pallas kernels for 0%

commit v1 on v0

--- a/solution.py
+++ b/solution.py
@@ -13,6 +13,27 @@
 beta_two = 0.6
 root_half = 0.7071067811865476
 inv_root_tau = 0.3989422804014327
+
+
+def collect(x, axis, dim):
+    size, here, width = (lax.axis_size(axis), lax.axis_index(axis), x.shape[dim])
+    upward = [(i, (i + 1) % size) for i in range(size)]
+    behind = [(i, (i - 1) % size) for i in range(size)]
+    out = jnp.zeros((*x.shape[:dim], size * width, *x.shape[dim + 1 :]), x.dtype)
+    out = lax.dynamic_update_slice_in_dim(out, x, here * width, axis=dim)
+    from_left = from_right = x
+    halfway = size // 2
+    for step in range(1, halfway + 1):
+        from_left = lax.ppermute(from_left, axis, upward)
+        out = lax.dynamic_update_slice_in_dim(
+            out, from_left, (here - step) % size * width, axis=dim
+        )
+        if step < size - halfway:
+            from_right = lax.ppermute(from_right, axis, behind)
+            out = lax.dynamic_update_slice_in_dim(
+                out, from_right, (here + step) % size * width, axis=dim
+            )
+    return out
 
 
 def rotary_tables(length, rot_dims):
@@ -138,7 +159,7 @@
     capacity = master.shape[1]
     block_width = master.shape[2]
     block_count = block_slot.shape[0]
-    copies = lax.all_gather(master[0].astype(jnp.bfloat16), "dp", axis=0, tiled=True)
+    copies = collect(master[0].astype(jnp.bfloat16), "dp", 0)
     flat_params = copies[block_slot].reshape(-1)
     w_qkv, w_out, w_up, w_down, norm_local = unpack(
         flat_params, d_model, heads_local, ff_local, width_local

time: 1460 us -> 1410 us (0.966)
  waiting for transfers between devices: 339 us -> 244 us
  local copies, waits for them, and re-layouts: 273 us -> 302 us
  starting transfers between devices: 0.73 us -> 20.1 us
    all_gather x1 -> x0, waiting for transfers between devices: 149 us -> none  [on_device(): lax.all_gather(master[0].astype(jnp.bfloat16), 'dp', axis=0, tiled=True)]
    ppermute x0 -> x7, waiting for transfers between devices: none -> 64 us  [the longest x4 63.9 us: collect(): from_left = lax.ppermute(from_left, axis, upward)]
    dynamic_update_slice x0 -> x8, local copies, waits for them, and re-layouts: none -> 35.4 us  [the longest x4 17.6 us: collect(): lax.dynamic_update_slice_in_dim(out, from_left, (here - step) % size * wi...]
    ppermute x0 -> x7, starting transfers between devices: none -> 19.4 us  [the longest x4 10.5 us: collect(): from_left = lax.ppermute(from_left, axis, upward)]
  transfers between devices with their start and end apart: 8 -> 14, of which waited for: 4 -> 5; matrix products, arithmetic and copies ran while one was open for 31% -> 34% of each run, Pallas kernels for 0% -> 0%
where the time goes in v1:
time: 1410 us; the launch traced here: 1400 us
  matrix products  625 us (44%)
  local copies, waits for them, and re-layouts  302 us (21%)
  waiting for transfers between devices  244 us (17%)
  other arithmetic  168 us (12%)
  starting transfers between devices  20.1 us (1%)
  loops' own time  16.5 us (1%)
  between operations  15.4 us (1%)
    psum x1, waiting for transfers between devices, on_device(): summed = lax.psum(grad_rows, 'dp')  158 us
    dot_general x1, matrix products, on_device(): clipped = jnp.dot(clip_scale, group_grads, precision=lax.Precision.HIGHEST)  119 us
    dot_general x8, matrix products, scores_of(): jnp.einsum('sqhd,skhd->shqk', query_block, key_rows, preferred_element_ty...  93.7 us
    unnamed x100, local copies, waits for them, and re-layouts  76.1 us
    dot_general x4, matrix products, backward_block(): jnp.einsum('sqhd,skhd->shqk', grad_block, values, preferred_element_type=...  72.5 us
    convert_element_type x4, other arithmetic, backward_block(): grad_scores = (probs * (grad_probs - row_dot)).astype(jnp.bfloat16)  68.2 us
    scatter x1, local copies, waits for them, and re-layouts, on_device(): slot_block = jnp.full((slot_total,), -1, jnp.int32).at[block_slot].set(jn...  65.6 us
    ppermute x4, waiting for transfers between devices, collect(): from_left = lax.ppermute(from_left, axis, upward)  63.9 us
  transfers between devices with their start and end apart: 14, of which 5 were waited for; matrix products, arithmetic and copies ran while one was open for 34% of the time, Pallas kernels for 0%

profile of v1, /device:TPU:0, one launch (start us, length us, event | category | flops | bytes accessed | tf_op | source)
XLA Modules:
  0.0 1401.6 jit_solution(11389081949527109156)
XLA Ops:
  15.5 25.4 %collective-permute-done = bf16[2594,128]{1,0:T(8,128)(2,1)S(1)} collective-permute-done((bf16[2594,128]{1,0:T(8,128)(2,1)S(1)}, bf16[2594,128]{1,0:T(8,128)(2,1)S(1)}, u32[]{:S(2)}, u32[]{:S(2)}) %collective-permute-start) | collective-permute-done | bytes 664096 | tf_op jit(solution)/shard_map/ppermute | solution.py:27
  54.9 16.2 %collective-permute-done.2 = bf16[2594,128]{1,0:T(8,128)(2,1)S(1)} collective-permute-done((bf16[2594,128]{1,0:T(8,128)(2,1)S(1)}, bf16[2594,128]{1,0:T(8,128)(2,1)S(1)}, u32[]{:S(2)}, u32[]{:S(2)}) %collective-permute-start.2) | collective-permute-done | bytes 664096 | tf_op jit(solution)/shard_map/ppermute | solution.py:27
  78.0 22.4 %collective-permute-done.4 = bf16[2594,128]{1,0:T(8,128)(2,1)S(1)} collective-permute-done((bf16[2594,128]{1,0:T(8,128)(2,1)S(1)}, bf16[2594,128]{1,0:T(8,128)(2,1)S(1)}, u32[]{:S(2)}, u32[]{:S(2)}) %collective-permute-start.4) | collective-permute-done | bytes 664096 | tf_op jit(solution)/shard_map/ppermute | solution.py:27
  135.4 29.7 %gather_fusion = bf16[13830,128]{1,0:T(8,128)(2,1)S(1)} fusion(bf16[20752,128]{1,0:T(8,128)(2,1)} %dynamic_update_slice.42, s32[14336]{0:T(1024)} %pad_clamp_fusion), kind=kCustom, calls=%fused_computation | custom fusion | bytes 7136280 | tf_op jit(solution)/shard_map/gather | solution.py:163
  194.7 7.9 fusion.36
  209.8 6.1 fusion.55
  225.8 163.2 %while.30 = (s32[]{:T(128)}, bf16[4,2,512,3,64]{2,4,3,1,0:T(8,128)(2,1)}, f32[4,2,3,512,1]{3,2,1,4,0:T(4,128)S(1)}, s32[4]{0:T(128)S(1)}, bf16[2,2048,3,64]{1,3,...) while((s32[]{:T(128)}, ...), condition=%wide.region_5.6_spmd.clone.clone, body=%wide.region_2.5_spmd.clone.sunk.clone | while | flops 1687156224 | bytes 96723152 | solution.py:214
  229.7 12.1 fusion.179
  241.8 12.1 fusion.180
  253.9 11.6 fusion.181
  270.5 12.1 fusion.179
  282.6 12.1 fusion.180
  294.7 11.6 fusion.181
  311.3 12.1 fusion.179
  323.4 12.1 fusion.180
  335.5 11.6 fusion.181
  352.1 12.1 fusion.179
  364.2 12.1 fusion.180
  376.3 11.6 fusion.181
  389.0 336.3 %while.31 = (s32[]{:T(128)}, f32[2,2048,3,64]{1,3,2,0:T(8,128)}, f32[2,2048,3,64]{1,3,2,0:T(8,128)}, f32[4,2,512,3,64]{2,4,3,1,0:T(8,128)}, s32[4]{0:T(128)S(1)}...) while((s32[]{:T(128)}, f32[2,2048,3,64]{1,3,2,0:T(8,128)}, ...), condition=%wide.region_9.10_spmd.clone.clone, body=%wide.region_7.9_spmd.clone.sunk.clone | while | flops 4126078464 | bytes 275603712 | solution.py:270
  393.2 11.3 fusion.191
  404.5 12.9 bitcast_add_fusion.7
  417.4 18.1 %multiply_reduce_fusion.4 = (f32[2,3,512]{2,1,0:T(4,128)S(1)}, f32[2,3,512,2048]{3,2,1,0:T(8,128)}) fusion(f32[2,3,512,2048]{3,2,1,0:T(8,128)} %fusion.191, f32[2,3,512]{2,1,0:T(4,128)S(1)} %dynamic-slice_bitcast_fusion.3, pred[512,2048]{1,0:T(8,128)(4,1)S(1)} %iota_compare_fusion.12, bf16[2,2048,3,64]{1,3,2,0:T(8,128)(2,1)} %copy-done.1, ...), kind=kOutput, calls=%fused_computation.22.clone.1.clone | convolution fusion | flops 836760576 | bytes 53370884 | tf_op jit(solution)/shard_map/while/body/eval_jaxpr/sqhd,skhd->shqk/dot_general | solution.py:245
  435.6 17.0 %multiply_convert_fusion.3 = bf16[2,3,512,2048]{3,2,1,0:T(8,128)(2,1)S(1)} fusion(f32[2,3,512,2048]{3,2,1,0:T(8,128)} %get-tuple-element.403, f32[2,3,512,2048]{3,2,1,0:T(8,128)} %fusion.191, f32[2,3,512]{2,1,0:T(4,128)S(1)} %get-tuple-element.404, f32[2,3,512]{2,1,0:T(4,128)S(1)} %dynamic-slice_bitcast_fusion.3, ...), kind=kLoop, calls=%fused_computation.21.clone.1.clone | loop fusion | flops 37748736 | bytes 63987712 | tf_op jit(solution)/shard_map/while/body/eval_jaxpr/convert_element_type | solution.py:249
  462.2 9.5 fusion.192
  475.7 11.3 fusion.191
  487.0 13.8 bitcast_add_fusion.7
  500.8 18.1 %multiply_reduce_fusion.4 = (f32[2,3,512]{2,1,0:T(4,128)S(1)}, f32[2,3,512,2048]{3,2,1,0:T(8,128)}) fusion(f32[2,3,512,2048]{3,2,1,0:T(8,128)} %fusion.191, f32[2,3,512]{2,1,0:T(4,128)S(1)} %dynamic-slice_bitcast_fusion.3, pred[512,2048]{1,0:T(8,128)(4,1)S(1)} %iota_compare_fusion.12, bf16[2,2048,3,64]{1,3,2,0:T(8,128)(2,1)} %copy-done.1, ...), kind=kOutput, calls=%fused_computation.22.clone.1.clone | convolution fusion | flops 836760576 | bytes 53370884 | tf_op jit(solution)/shard_map/while/body/eval_jaxpr/sqhd,skhd->shqk/dot_general | solution.py:245
  518.9 17.0 %multiply_convert_fusion.3 = bf16[2,3,512,2048]{3,2,1,0:T(8,128)(2,1)S(1)} fusion(f32[2,3,512,2048]{3,2,1,0:T(8,128)} %get-tuple-element.403, f32[2,3,512,2048]{3,2,1,0:T(8,128)} %fusion.191, f32[2,3,512]{2,1,0:T(4,128)S(1)} %get-tuple-element.404, f32[2,3,512]{2,1,0:T(4,128)S(1)} %dynamic-slice_bitcast_fusion.3, ...), kind=kLoop, calls=%fused_computation.21.clone.1.clone | loop fusion | flops 37748736 | bytes 63987712 | tf_op jit(solution)/shard_map/while/body/eval_jaxpr/convert_element_type | solution.py:249
  540.5 6.1 bitcast_add_fusion.6
  546.6 9.6 fusion.192
  560.1 11.3 fusion.191
  571.5 13.8 bitcast_add_fusion.7
  585.3 18.1 %multiply_reduce_fusion.4 = (f32[2,3,512]{2,1,0:T(4,128)S(1)}, f32[2,3,512,2048]{3,2,1,0:T(8,128)}) fusion(f32[2,3,512,2048]{3,2,1,0:T(8,128)} %fusion.191, f32[2,3,512]{2,1,0:T(4,128)S(1)} %dynamic-slice_bitcast_fusion.3, pred[512,2048]{1,0:T(8,128)(4,1)S(1)} %iota_compare_fusion.12, bf16[2,2048,3,64]{1,3,2,0:T(8,128)(2,1)} %copy-done.1, ...), kind=kOutput, calls=%fused_computation.22.clone.1.clone | convolution fusion | flops 836760576 | bytes 53370884 | tf_op jit(solution)/shard_map/while/body/eval_jaxpr/sqhd,skhd->shqk/dot_general | solution.py:245
  603.4 17.0 %multiply_convert_fusion.3 = bf16[2,3,512,2048]{3,2,1,0:T(8,128)(2,1)S(1)} fusion(f32[2,3,512,2048]{3,2,1,0:T(8,128)} %get-tuple-element.403, f32[2,3,512,2048]{3,2,1,0:T(8,128)} %fusion.191, f32[2,3,512]{2,1,0:T(4,128)S(1)} %get-tuple-element.404, f32[2,3,512]{2,1,0:T(4,128)S(1)} %dynamic-slice_bitcast_fusion.3, ...), kind=kLoop, calls=%fused_computation.21.clone.1.clone | loop fusion | flops 37748736 | bytes 63987712 | tf_op jit(solution)/shard_map/while/body/eval_jaxpr/convert_element_type | solution.py:249
  625.0 6.1 bitcast_add_fusion.6
  631.1 9.5 fusion.192
  644.6 11.3 fusion.191
  655.9 13.8 bitcast_add_fusion.7
  669.6 18.1 %multiply_reduce_fusion.4 = (f32[2,3,512]{2,1,0:T(4,128)S(1)}, f32[2,3,512,2048]{3,2,1,0:T(8,128)}) fusion(f32[2,3,512,2048]{3,2,1,0:T(8,128)} %fusion.191, f32[2,3,512]{2,1,0:T(4,128)S(1)} %dynamic-slice_bitcast_fusion.3, pred[512,2048]{1,0:T(8,128)(4,1)S(1)} %iota_compare_fusion.12, bf16[2,2048,3,64]{1,3,2,0:T(8,128)(2,1)} %copy-done.1, ...), kind=kOutput, calls=%fused_computation.22.clone.1.clone | convolution fusion | flops 836760576 | bytes 53370884 | tf_op jit(solution)/shard_map/while/body/eval_jaxpr/sqhd,skhd->shqk/dot_general | solution.py:245
  687.8 17.0 %multiply_convert_fusion.3 = bf16[2,3,512,2048]{3,2,1,0:T(8,128)(2,1)S(1)} fusion(f32[2,3,512,2048]{3,2,1,0:T(8,128)} %get-tuple-element.403, f32[2,3,512,2048]{3,2,1,0:T(8,128)} %fusion.191, f32[2,3,512]{2,1,0:T(4,128)S(1)} %get-tuple-element.404, f32[2,3,512]{2,1,0:T(4,128)S(1)} %dynamic-slice_bitcast_fusion.3, ...), kind=kLoop, calls=%fused_computation.21.clone.1.clone | loop fusion | flops 37748736 | bytes 63987712 | tf_op jit(solution)/shard_map/while/body/eval_jaxpr/convert_element_type | solution.py:249
  715.4 9.5 fusion.192
  738.2 9.5 copy.55
  763.4 9.7 fusion.109
  778.6 9.4 convolution_convert_fusion
  790.4 33.4 %fusion.41 = (bf16[4096,768]{1,0:T(8,128)(2,1)}, f32[4096,768]{1,0:T(8,128)S(1)}) fusion(bf16[4096,768]{1,0:T(8,128)(2,1)} %get-tuple-element.237, bf16[768,768]{1,0:T(8,128)(2,1)S(1)} %copy-done.22), kind=kOutput, calls=%fused_computation.59 | convolution fusion | flops 5036310528 | bytes 26345472 | tf_op jit(solution)/shard_map/dot_general | solution.py:216
  823.8 9.2 fusion.47
  835.5 7.0 convolution_convert_fusion.1
  842.6 9.4 convolution_bitcast_fusion.1
  858.9 6.2 constant_dynamic-update-slice_fusion.2
  867.5 12.3 convolution_bitcast_fusion
  879.9 11.6 fusion.108
  896.8 21.4 %reduce-scatter.11.cloned.1.call-done = bf16[1024,768]{1,0:T(8,128)(2,1)} async-done(((bf16[4096,768]{1,0:T(8,128)(2,1)}), bf16[1024,768]{1,0:T(8,128)(2,1)}) %reduce-scatter.11.cloned.1.call-update) | async-done | bytes 1572880 | tf_op jit(solution)/shard_map/reduce_scatter | solution.py:293
  927.2 9.1 add_convert_fusion
  936.3 8.1 copy.83
  952.5 41.5 %multiply_reduce_fusion.1 = (f32[2]{0:T(128)S(1)}, f32[2,1770240]{1,0:T(2,128)}) fusion(f32[2,1770240]{1,0:T(2,128)} %constant_dynamic-update-slice_fusion, s32[2]{0:T(128)S(1)} %copy-done.37), kind=kOutput, calls=%fused_computation.55 | convolution fusion | flops 92052480 | bytes 28323856 | tf_op jit(solution)/shard_map/dot_general | solution.py:337
  994.0 6.4 psum.14
  1000.4 119.3 %convolution_reduce_fusion = f32[1770240]{0:T(1024)} fusion(f32[2,1770240]{1,0:T(2,128)} %get-tuple-element.257, f32[2]{0:T(128)S(1)} %sqrt.7), kind=kOutput, calls=%fused_computation.115 | convolution fusion | flops 42485764 | bytes 21242888 | tf_op jit(solution)/shard_map/dot_general | solution.py:341
  1119.7 65.6 %scatter_custom_fusion = s32[20752]{0:T(1024)S(1)} fusion(s32[13830]{0:T(1024)} %copy-done.27, s32[13830]{0:T(1024)S(1)} %iota.92, s32[]{:T(128)} %constant.109.clone.1), kind=kCustom, calls=%fused_computation.159 | custom fusion | bytes 83520 | tf_op jit(solution)/shard_map/scatter | solution.py:347
  1196.9 157.6 %all-reduce.2.cloned.1.call-done = f32[13830,128]{1,0:T(8,128)} async-done(((f32[13830,128]{1,0:T(8,128)}), f32[13830,128]{1,0:T(8,128)}) %all-reduce.2.cloned.1.call-update) | async-done | bytes 7080976 | tf_op jit(solution)/shard_map/psum | solution.py:350
  1354.5 7.7 gather_fusion.1
  1367.4 9.0 copy.67
  1376.4 9.0 copy.69
  1385.4 9.0 copy.68
  (289 shorter events, 247.0 us)
Async XLA Ops:
  7.2 181.0 %all-gather.4.cloned.1.call-start = ((), (), s32[]{:S(2)}) async-start(), calls=%async_computation.4 | async-start | bytes 7864320 | tf_op jit(solution)/shard_map/all_gather | solution.py:168
  7.9 201.9 %all-gather.6.cloned.1.call-start = ((), (), s32[]{:S(2)}) async-start(), calls=%async_computation.6 | async-start | bytes 7864320 | tf_op jit(solution)/shard_map/all_gather | solution.py:225
  9.3 65.5 %copy-start.35 = (s32[13830]{0:T(1024)S(1)}, s32[13830]{0:T(1024)}, u32[]{:S(2)}) copy-start(s32[13830]{0:T(1024)} %param.14) | copy-start | bytes 165964
  9.4 31.5 %collective-permute-start = (bf16[2594,128]{1,0:T(8,128)(2,1)S(1)}, bf16[2594,128]{1,0:T(8,128)(2,1)S(1)}, u32[]{:S(2)}, u32[]{:S(2)}) collective-permute-start(bf16[2594,128]{1,0:T(8,128)(2,1)S(1)} %bitcast.229), channel_id=1, source_target_pairs={{0,4},{4,8},{8,12},{12,16},{16,20},{20,24},{24,28},{28,0},{1,5},{5... | collective-permute-start | bytes 1992200 | tf_op jit(solution)/shard_map/ppermute | solution.py:27
  12.4 39.8 %collective-permute-start.1 = (bf16[2594,128]{1,0:T(8,128)(2,1)S(1)}, bf16[2594,128]{1,0:T(8,128)(2,1)S(1)}, u32[]{:S(2)}, u32[]{:S(2)}) collective-permute-start(bf16[2594,128]{1,0:T(8,128)(2,1)S(1)} %bitcast.230), channel_id=1, source_target_pairs={{0,28},{4,0},{8,4},{12,8},{16,12},{20,16},{24,20},{28,24},{1,29},{... | collective-permute-start | bytes 1992200 | tf_op jit(solution)/shard_map/ppermute | solution.py:32
  40.8 30.2 %collective-permute-start.2 = (bf16[2594,128]{1,0:T(8,128)(2,1)S(1)}, bf16[2594,128]{1,0:T(8,128)(2,1)S(1)}, u32[]{:S(2)}, u32[]{:S(2)}) collective-permute-start(bf16[2594,128]{1,0:T(8,128)(2,1)S(1)} %collective-permute-done), channel_id=1, source_target_pairs={{0,4},{4,8},{8,12},{12,16},{16,20},{20,24},{24,28},{28,0},{1,5},{5... | collective-permute-start | bytes 1992200 | tf_op jit(solution)/shard_map/ppermute | solution.py:27
  43.4 848.1 %reduce-scatter.9.cloned.1.call-start = ((), (), s32[]{:S(2)}) async-start(), calls=%async_computation.7 | async-start | bytes 7864320 | tf_op jit(solution)/shard_map/reduce_scatter | solution.py:290
  52.1 22.8 %collective-permute-start.3 = (bf16[2594,128]{1,0:T(8,128)(2,1)S(1)}, bf16[2594,128]{1,0:T(8,128)(2,1)S(1)}, u32[]{:S(2)}, u32[]{:S(2)}) collective-permute-start(bf16[2594,128]{1,0:T(8,128)(2,1)S(1)} %collective-permute-done.1), channel_id=1, source_target_pairs={{0,28},{4,0},{8,4},{12,8},{16,12},{20,16},{24,20},{28,24},{1,29},{... | collective-permute-start | bytes 1992200 | tf_op jit(solution)/shard_map/ppermute | solution.py:32
  71.1 29.3 %collective-permute-start.4 = (bf16[2594,128]{1,0:T(8,128)(2,1)S(1)}, bf16[2594,128]{1,0:T(8,128)(2,1)S(1)}, u32[]{:S(2)}, u32[]{:S(2)}) collective-permute-start(bf16[2594,128]{1,0:T(8,128)(2,1)S(1)} %collective-permute-done.2), channel_id=1, source_target_pairs={{0,4},{4,8},{8,12},{12,16},{16,20},{20,24},{24,28},{28,0},{1,5},{5... | collective-permute-start | bytes 1992200 | tf_op jit(solution)/shard_map/ppermute | solution.py:27
  74.9 28.0 %copy-start.27 = (s32[13830]{0:T(1024)}, s32[13830]{0:T(1024)S(1)}, u32[]{:S(2)}) copy-start(s32[13830]{0:T(1024)S(1)} %compare_select_fusion) | copy-start | bytes 165964
  74.9 51.4 %collective-permute-start.5 = (bf16[2594,128]{1,0:T(8,128)(2,1)S(1)}, bf16[2594,128]{1,0:T(8,128)(2,1)}, u32[]{:S(2)}, u32[]{:S(2)}) collective-permute-start(bf16[2594,128]{1,0:T(8,128)(2,1)S(1)} %collective-permute-done.3), channel_id=1, source_target_pairs={{0,28},{4,0},{8,4},{12,8},{16,12},{20,16},{24,20},{28,24},{1,29},{... | collective-permute-start | bytes 1992200 | tf_op jit(solution)/shard_map/ppermute | solution.py:32
  100.4 30.4 %collective-permute-start.6 = (bf16[2594,128]{1,0:T(8,128)(2,1)S(1)}, bf16[2594,128]{1,0:T(8,128)(2,1)}, u32[]{:S(2)}, u32[]{:S(2)}) collective-permute-start(bf16[2594,128]{1,0:T(8,128)(2,1)S(1)} %collective-permute-done.4), channel_id=1, source_target_pairs={{0,4},{4,8},{8,12},{12,16},{16,20},{20,24},{24,28},{28,0},{1,5},{5... | collective-permute-start | bytes 1992200 | tf_op jit(solution)/shard_map/ppermute | solution.py:27
  174.4 20.3 %copy-start.31 = (f32[768]{0:T(1024)}, f32[768]{0:T(1024)S(1)}, u32[]{:S(2)}) copy-start(f32[768]{0:T(1024)S(1)} %mul.489) | copy-start | bytes 9220
  174.5 20.2 %copy-start.33 = (f32[768]{0:T(1024)}, f32[768]{0:T(1024)S(1)}, u32[]{:S(2)}) copy-start(f32[768]{0:T(1024)S(1)} %mul.505) | copy-start | bytes 9220
  180.1 6.2 copy-start.16
  185.6 6.3 copy-start.17
  188.1 4.6 copy-start.3
  194.7 7.9 copy-start.30
  202.5 3.9 copy-start.12
  219.3 3.6 copy-start.11
  219.3 3.8 copy-start.23
  219.3 3.8 copy-start.25
  241.8 12.1 copy-start.7
  282.6 12.1 copy-start.7
  323.4 12.1 copy-start.7
  364.2 12.1 copy-start.7
  389.2 3.3 copy-start.1
  452.6 4.5 copy-start
  462.2 9.5 copy-start.2
  536.0 4.5 copy-start
  546.6 9.6 copy-start.2
  556.2 3.3 copy-start.1
  620.4 4.5 copy-start
  631.1 9.6 copy-start.2
  704.8 4.5 copy-start
  715.4 9.5 copy-start.2
  725.3 4.1 copy-start.24
  725.3 4.1 copy-start.26
  738.2 9.5 copy-start.9
  748.9 9.3 slice-start
  751.4 6.7 slice-start.1
  756.2 7.2 slice-start.4
  758.2 5.2 slice-start.5
  788.0 130.3 %reduce-scatter.11.cloned.1.call-start = ((), (), s32[]{:S(2)}) async-start(), calls=%async_computation.8 | async-start | bytes 7864320 | tf_op jit(solution)/shard_map/reduce_scatter | solution.py:293
  788.1 35.7 %slice-start.2 = ((s8[6291456]{0:T(1024)(128)(4,1)}), s8[4194304]{0:T(1024)(128)(4,1)S(1)}, s32[]{:S(2)}) async-start(s8[6291456]{0:T(1024)(128)(4,1)} %bitcast.217), calls=%async_computation.13 | async-start | bytes 8388608
  790.4 33.4 %slice-start.3 = ((s8[6291456]{0:T(1024)(128)(4,1)}), s8[2097152]{0:T(1024)(128)(4,1)S(1)}, s32[]{:S(2)}) async-start(s8[6291456]{0:T(1024)(128)(4,1)} %bitcast.217), calls=%async_computation.14 | async-start | bytes 4194304
  790.4 33.4 %copy-start.20 = (bf16[768,768]{1,0:T(8,128)(2,1)S(1)}, bf16[768,768]{1,0:T(8,128)(2,1)}, u32[]{:S(2)}) copy-start(bf16[768,768]{1,0:T(8,128)(2,1)} %reshape.377) | copy-start | bytes 3538948
  852.0 5.8 copy-start.15
  858.9 91.7 %reduce-scatter.13.cloned.1.call-start = ((), (), s32[]{:S(2)}) async-start(), calls=%async_computation.10 | async-start | bytes 491520
  858.9 6.2 copy-start.10
  867.5 12.4 copy-start.21
  879.9 11.6 copy-start.28
  896.8 30.4 %copy-start.19 = (bf16[192,768]{1,0:T(8,128)(2,1)S(1)}, bf16[192,768]{1,0:T(8,128)(2,1)}, u32[]{:S(2)}) copy-start(bf16[192,768]{1,0:T(8,128)(2,1)} %reshape.375) | copy-start | bytes 884740
  918.3 3.8 copy-start.6
  926.8 262.1 %reduce-scatter.7.cloned.1.call-start = ((), (), s32[]{:S(2)}) async-start(), calls=%async_computation.5 | async-start | bytes 7864320 | tf_op jit(solution)/shard_map/reduce_scatter | solution.py:221
  944.4 410.1 %all-reduce.2.cloned.1.call-start = ((), (), s32[]{:S(2)}) async-start(), calls=%async_computation.9 | async-start | bytes 14163968 | tf_op jit(solution)/shard_map/psum | solution.py:350
  944.5 8.0 copy-start.37
  1000.4 119.3 %copy-start.40 = (f32[2]{0:T(128)}, f32[2]{0:T(128)S(1)}, u32[]{:S(2)}) copy-start(f32[2]{0:T(128)S(1)} %sqrt.7) | copy-start | bytes 28
  1119.7 65.9 %copy-start.5 = (bf16[1024,768]{1,0:T(8,128)(2,1)S(1)}, bf16[1024,768]{1,0:T(8,128)(2,1)}, u32[]{:S(2)}) copy-start(bf16[1024,768]{1,0:T(8,128)(2,1)} %reduce-scatter.9.cloned.1.call-done) | copy-start | bytes 4718596
  1119.7 65.9 %copy-start.32 = (f32[768]{0:T(1024)S(1)}, f32[768]{0:T(1024)}, u32[]{:S(2)}) copy-start(f32[768]{0:T(1024)} %copy-done.31) | copy-start | bytes 9220
  1119.7 65.9 %copy-start.34 = (f32[768]{0:T(1024)S(1)}, f32[768]{0:T(1024)}, u32[]{:S(2)}) copy-start(f32[768]{0:T(1024)} %copy-done.33) | copy-start | bytes 9220
  1185.5 7.0 dynamic-slice-start
  1188.9 3.6 copy-start.13
  1196.9 165.3 %copy-start.14 = (f32[1,2594,128]{2,0,1:T(1,128)S(1)}, f32[1,2594,128]{2,0,1:T(1,128)}, u32[]{:S(2)}) copy-start(f32[1,2594,128]{2,0,1:T(1,128)} %param.15) | copy-start | bytes 3984388
  (13 other events, 29.7 us)
Sparse Core Ops, SparseCore 0:
  9.5 49.0 all-gather.3
  60.2 46.3 all-gather.5
  788.1 59.2 reduce-scatter.8
  859.0 59.2 reduce-scatter.10
  926.9 20.8 reduce-scatter.12
  950.1 58.9 reduce-scatter.6
  1119.8 234.6 all-reduce.1
